TPU v7x, 32 devices: a whole 2x2x4 slice. The times are simulated.
32 devices in a mesh: groups: 2 (over x), blk: 16 (over z, y, core).
Axes of the slice: x: 2, y: 2, z: 4, core: 2. Of those that a mesh axis runs over, the one named last changes fastest.
Arguments:
- factors: bfloat16 [64, 2, 64, 128], P(('groups', 'blk')), parts along dimension 0, may hold values from -2.09375 to 2.09375
- token_mask: int32 [64, 64], P(('groups', 'blk')), parts along dimension 0, may hold values 0 or 1
- store: bfloat16 [16384, 2, 4096], P(('groups', 'blk')), parts along dimension 0, may hold values from -0.0625 to 0.0625
- inv_fisher: bfloat16 [2, 4096, 4096], P(None, 'blk'), as said below
- source_ids: int32 [16384], P(('groups', 'blk')), parts along dimension 0, may hold values from 0 to 15
- source_weight: float32 [16], replicated, may hold values from 0.25 to 4
Outputs:
- scores: float32 [64, 8192], P('groups', 'blk'), parts along dimension 0
There are 2 independent parts, one for each index of `groups`. A program takes and returns all parts, laid end to end along the dimension named above; an argument that names none is the same for every part. Nothing has to cross between parts.
Inputs may be any that keep to these rules, and one draw needn't show every extreme that they name: `inv_fisher`: each layer's matrix is symmetric.
All inputs are finite; a program needn't handle non-finite values. No bound on the sum of `token_mask` on one device may be relied on, other than what follows from the above.
Results may differ from a plain program's by a relative error of at most 0.004.
Values may be sent and summed in bfloat16 or wider, within the bound.
A program may use at most 64 MiB of HBM per device.

v0:
```python
import functools
import jax
import jax.numpy as jnp
from jax import lax
from jax.experimental import pallas as pl
from jax.experimental.pallas import tpu as pltpu
from jax.sharding import PartitionSpec as P

LANES = 128
NT = (((1,), (1,)), ((), ()))


def make_grads(factors, token_mask):
    rank_size = factors.shape[3] // 2
    mask_values = token_mask.astype(jnp.float32)[:, None, :, None]
    left_side = factors[..., :rank_size].astype(jnp.float32) * mask_values
    right_side = factors[..., rank_size:].astype(jnp.float32)
    outer_sum = jnp.einsum("qlta,qltb->qlab", left_side, right_side)
    return outer_sum.reshape(outer_sum.shape[0], outer_sum.shape[1], rank_size * rank_size).astype(
        jnp.bfloat16
    )


def scale_of(source_ids, source_weight):
    matches = (
        source_ids[:, None] == jnp.arange(source_weight.shape[0], dtype=jnp.int32)[None, :]
    ).astype(jnp.float32)
    return jnp.sum(matches * source_weight[None, :], axis=1)


def plain(factors, token_mask, store, inv_fisher, source_ids, source_weight):
    query_grads = make_grads(factors, token_mask)
    layer_count = inv_fisher.shape[0]
    segment = lax.all_gather(query_grads, "blk", axis=0, tiled=True)
    products = [
        lax.dot_general(
            segment[:, layer_idx], inv_fisher[layer_idx], NT, preferred_element_type=jnp.float32
        )
        for layer_idx in range(layer_count)
    ]
    hidden_cols = jnp.stack(products, axis=1).astype(jnp.bfloat16)
    hidden = lax.all_to_all(hidden_cols, "blk", split_axis=0, concat_axis=2, tiled=True)
    raw_scores = lax.dot_general(
        lax.all_gather(hidden, "blk", axis=0, tiled=True),
        store,
        (((1, 2), (1, 2)), ((), ())),
        preferred_element_type=jnp.float32,
    )
    return raw_scores * scale_of(source_ids, source_weight)[None, :]


class Gather:
    def __init__(self, buf, send_sems, recv_sems, sizes):
        self.buf, self.send_sems, self.recv_sems = buf, send_sems, recv_sems
        self.outer, self.ys, self.cores = sizes
        me = lax.axis_index("blk")
        self.me = me
        self.c = lax.rem(me, self.cores)
        self.y = lax.rem(me // self.cores, self.ys)
        self.z = me // (self.cores * self.ys)
        self.sent = []

    def index(self, dz, dy, dc):
        if self.outer & (self.outer - 1):
            z = lax.rem(self.z + dz, self.outer)
        else:
            z, bit = self.z, 1
            while bit <= dz:
                if dz & bit:
                    z = z + bit - 2 * bit * lax.rem(z // bit, 2)
                bit *= 2
        y = lax.rem(self.y + dy, self.ys)
        c = lax.rem(self.c + dc, self.cores)
        return (z * self.ys + y) * self.cores + c

    def copy(self, slot, target, count):
        return pltpu.make_async_remote_copy(
            src_ref=self.buf.at[slot],
            dst_ref=self.buf.at[slot],
            send_sem=self.send_sems.at[count],
            recv_sem=self.recv_sems.at[slot],
            device_id={"blk": target},
            device_id_type=pl.DeviceIdType.MESH,
        )

    def send(self, slot, target):
        one = self.copy(slot, target, len(self.sent))
        one.start()
        self.sent.append(one)

    def arrive(self, slot):
        self.copy(slot, self.me, 0).wait_recv()

    def z_peers(self):
        return [self.index(k, 0, 0) for k in range(self.outer - 1, 0, -1)]

    def y_peers(self):
        return [self.index(0, k, 0) for k in range(1, self.ys)]

    def c_peers(self):
        return [self.index(0, 0, k) for k in range(1, self.cores)]

    def peers(self):
        return self.z_peers() + self.y_peers() + self.c_peers()

    def start(self):
        for target in self.z_peers() + self.y_peers() + self.c_peers():
            self.send(self.me, target)

    def z_slots(self):
        return [self.index(k, 0, 0) for k in range(1, self.outer)]

    def y_slots(self):
        return [self.index(k, j, 0) for k in range(self.outer) for j in range(1, self.ys)]

    def c_slots(self, near):
        return [
            self.index(k, j, i)
            for i in range(1, self.cores)
            for j in range(self.ys)
            for k in range(self.outer)
            if (j == 0) == near
        ]

    def take_z(self, slot):
        self.arrive(slot)
        for target in self.y_peers() + self.c_peers():
            self.send(slot, target)

    def take_y(self, slot):
        self.arrive(slot)
        for target in self.c_peers():
            self.send(slot, target)

    def finish(self):
        for one in self.sent:
            one.wait_send()


def kernel(
    sizes, mask_ref, factors_ref, ids_ref, weight_ref, fisher_hbm, store_hbm, out_ref,
    fisher, store, grads, hidden, spread, lhs, total, turned,
    send_sems, recv_sems, fisher_sems, store_sem,
):
    nq, layers, _, width = factors_ref.shape
    rank = width // 2
    rows = rank * rank // LANES
    n = grads.shape[1]
    m = n * nq
    per = hidden.shape[3] // LANES
    train = out_ref.shape[1]

    gathers = [
        [
            Gather(buf.at[l], send_sems.at[p, l], recv_sems.at[p, l], sizes)
            for l in range(layers)
        ]
        for p, buf in enumerate((grads, hidden))
    ]
    first = gathers[0][0]
    me = first.me
    barrier = pltpu.get_barrier_semaphore()
    peers = first.peers()
    for peer in peers:
        pl.semaphore_signal(
            barrier, inc=1, device_id={"blk": peer}, device_id_type=pl.DeviceIdType.MESH
        )
    fisher_copies = [
        pltpu.make_async_copy(fisher_hbm.at[l], fisher.at[l], fisher_sems.at[l])
        for l in range(layers)
    ]
    for one in fisher_copies:
        one.start()
    for fb in range(store.shape[0]):
        pltpu.make_async_copy(
            store_hbm.at[:, :, fb * LANES : (fb + 1) * LANES], store.at[fb], store_sem
        ).start()

    row = lax.broadcasted_iota(jnp.int32, (rows, width), 0)
    lane = lax.broadcasted_iota(jnp.int32, (rows, width), 1)
    picks = [(lane == 2 * row + par).astype(jnp.bfloat16) for par in range(2)]
    for l in range(layers):
        for q in range(nq):
            block = factors_ref[q, l]
            wide = block.astype(jnp.float32)
            high = lax.broadcasted_iota(jnp.int32, wide.shape, 1) >= rank
            rights = [
                jnp.where(high, 0.0, pltpu.roll(wide, rank, 1)).astype(jnp.bfloat16),
                jnp.where(high, wide, 0.0).astype(jnp.bfloat16),
            ]
            keep = mask_ref[q : q + 1, :].astype(jnp.float32)
            grad = None
            for par in range(2):
                left = lax.dot_general(picks[par], block, NT, preferred_element_type=jnp.float32)
                left = (left * keep).astype(jnp.bfloat16)
                term = jnp.dot(left, rights[par], preferred_element_type=jnp.float32)
                grad = term if grad is None else grad + term
            grads[l, me, q * rows : (q + 1) * rows, :] = grad.astype(jnp.bfloat16)
        if l == 0:
            pl.semaphore_wait(barrier, len(peers))
        gathers[0][l].start()
    ids = ids_ref[...]
    scale = jnp.zeros(ids.shape, jnp.float32)
    for source in range(weight_ref.shape[0]):
        scale = scale + jnp.where(ids == source, weight_ref[source], 0.0)

    def place(l, slot):
        for q in range(nq):
            spread[l, pl.ds(slot * nq + q, rows, stride=m), :] = grads[
                l, slot, q * rows : (q + 1) * rows, :
            ].astype(jnp.float32)

    for l in range(layers):
        place(l, me)
    for l in range(layers):
        one = gathers[0][l]
        for slot in one.z_slots():
            one.take_z(slot)
            place(l, slot)
    for l in range(layers):
        one = gathers[0][l]
        for slot in one.y_slots():
            one.take_y(slot)
            place(l, slot)
    for l in range(layers):
        one = gathers[0][l]
        for slot in one.c_slots(True):
            one.arrive(slot)
            place(l, slot)

    for l in range(layers):
        for slot in gathers[0][l].c_slots(False):
            gathers[0][l].arrive(slot)
            place(l, slot)
        for r in range(rows):
            lhs[:, r * LANES : (r + 1) * LANES] = spread[l, r * m : (r + 1) * m, :].astype(
                jnp.bfloat16
            )
        fisher_copies[l].wait()
        product = lax.dot_general(lhs[...], fisher[l], NT, preferred_element_type=jnp.float32)
        hidden[l, me] = product.astype(jnp.bfloat16)
        gathers[1][l].start()

    pltpu.make_async_copy(store, store, store_sem).wait()
    flat = store.reshape(store.shape[0], train * layers, LANES)

    def add(slot, fresh=False):
        left = jnp.concatenate([hidden[l, slot] for l in range(layers)], axis=0)
        right = jnp.concatenate([flat[slot * per + i] for i in range(per)], axis=1)
        term = lax.dot_general(left, right, NT, preferred_element_type=jnp.float32)
        total[...] = term if fresh else total[...] + term

    add(me, True)
    pair = gathers[1]
    slots = pair[0].z_slots()
    for one in pair[:-1]:
        for slot in slots:
            one.take_z(slot)
    for slot in slots:
        pair[-1].take_z(slot)
        add(slot)
    early = pair[0].c_slots(True)
    slots = pair[0].y_slots()
    for at in range(max(len(slots), len(early))):
        for slot in slots[at : at + 1]:
            for one in pair:
                one.take_y(slot)
            add(slot)
        for slot in early[at : at + 1]:
            for one in pair:
                one.arrive(slot)
            add(slot)
    for slot in pair[0].c_slots(False):
        for one in pair:
            one.arrive(slot)
        add(slot)

    turned[:, : layers * m] = total[...].T
    answer = None
    for l in range(layers):
        part = turned[pl.ds(l, train, stride=layers), :][:, l * m : (l + 1) * m]
        answer = part if answer is None else answer + part
    out_ref[...] = answer.T * scale
    for some in gathers:
        for one in some:
            one.finish()


def fused(n, factors, token_mask, store, inv_fisher, source_ids, source_weight):
    nq, layers, _, width = factors.shape
    train, _, feat = store.shape
    cols = inv_fisher.shape[1]
    m = n * nq
    rows = feat // LANES
    cores = 2 if n % 2 == 0 else 1
    ys = 2 if n % 4 == 0 else 1
    sizes = (n // (cores * ys), ys, cores)
    anyspace = pl.BlockSpec(memory_space=pl.ANY)
    vmem = pl.BlockSpec(memory_space=pltpu.VMEM)
    return pl.pallas_call(
        functools.partial(kernel, sizes),
        out_shape=pltpu.VMEM((m, train), jnp.float32),
        in_specs=[
            vmem, vmem, vmem, pl.BlockSpec(memory_space=pltpu.SMEM), anyspace, anyspace
        ],
        out_specs=vmem,
        scratch_shapes=[
            pltpu.VMEM((layers, cols, feat), jnp.bfloat16),
            pltpu.VMEM((rows, train, layers, LANES), jnp.bfloat16),
            pltpu.VMEM((layers, n, nq * rows, LANES), jnp.bfloat16),
            pltpu.VMEM((layers, n, m, cols), jnp.bfloat16),
            pltpu.VMEM((layers, rows * m, LANES), jnp.float32),
            pltpu.VMEM((m, feat), jnp.bfloat16),
            pltpu.VMEM((layers * m, train * layers), jnp.float32),
            pltpu.VMEM((train * layers, LANES), jnp.float32),
            pltpu.SemaphoreType.DMA((2, layers, n)),
            pltpu.SemaphoreType.DMA((2, layers, n)),
            pltpu.SemaphoreType.DMA((layers,)),
            pltpu.SemaphoreType.DMA(()),
        ],
        compiler_params=pltpu.CompilerParams(
            collective_id=0, has_side_effects=True, vmem_limit_bytes=60 * 2**20
        ),
        name="scores",
    )(token_mask, factors, source_ids[None, :], source_weight, inv_fisher, store)


def local(n, factors, token_mask, store, inv_fisher, source_ids, source_weight):
    nq, layers, _, width = factors.shape
    train, _, feat = store.shape
    cols = inv_fisher.shape[1]
    m = n * nq
    held = 2 * (inv_fisher.size + store.size) + 4 * layers * m * train * layers
    fits = (
        width == LANES
        and feat * 4 == width * width
        and cols % LANES == 0
        and layers == 2
        and m % 16 == 0
        and layers * m <= LANES
        and train % LANES == 0
        and held < 40 * 2**20
    )
    if not fits:
        return plain(factors, token_mask, store, inv_fisher, source_ids, source_weight)
    return fused(n, factors, token_mask, store, inv_fisher, source_ids, source_weight)


def solution(mesh):
    placed = (
        P(("groups", "blk"), None, None, None),
        P(("groups", "blk"), None),
        P(("groups", "blk"), None, None),
        P(None, "blk", None),
        P(("groups", "blk")),
        P(),
    )
    return jax.shard_map(
        functools.partial(local, mesh.shape["blk"]),
        mesh=mesh, in_specs=placed, out_specs=P("groups", "blk"), check_vma=False,
    )
```

profile of v0, /device:TPU:0, one launch (start us, length us, event | category | flops | bytes accessed | tf_op | source)
XLA Modules:
  0.0 26.9 jit_solution(9123594068574243146)
XLA Ops:
  0.0 26.3 %scores.1 = f32[32,512]{1,0:T(8,128)S(1)} custom-call(s32[2,64]{1,0:T(2,128)} %mask_ref.1, bf16[2,2,64,128]{3,2,1,0:T(8,128)(2,1)} %factors_ref.1, s32[1,512]{1,0:T(1,128)} %bitcast.1, f32[16]{0:T(128)} %weight_ref.1, bf16[2,256,4096]{2,1,0:T(8,128)(2,1)} %fisher_hbm.1, bf16[512,2,4096]{2,1,0:T(2,128)(2,1)} %store_hbm.1), custom_call_target="tpu_custom_call" | custom-call | tf_op jit(solution)/shard_map/scores/pallas_call | solution.py:300
  26.3 0.6 %copy.8 = f32[32,512]{1,0:T(8,128)} copy(f32[32,512]{1,0:T(8,128)S(1)} %scores.1) | data formatting | bytes 131072
where the time goes:
time: 27.1 us; the launch traced here: 26.9 us
  Pallas kernels  26.3 us (97%)
  local copies, waits for them, and re-layouts  0.63 us (2%)
    pallas_call x1, Pallas kernels, fused(): pl.pallas_call(functools.partial(kernel, sizes), out_shape=pltpu.VMEM((m,...  26.3 us
    unnamed x1, local copies, waits for them, and re-layouts  0.63 us

commit v1 on v0

--- a/solution.py
+++ b/solution.py
@@ -138,16 +138,16 @@
 
 
 def kernel(
-    sizes, mask_ref, factors_ref, ids_ref, weight_ref, fisher_hbm, store_hbm, out_ref,
+    sizes, mask_hbm, factors_hbm, ids_hbm, weight_hbm, fisher_hbm, store_hbm, out_ref,
+    mask_ref, factors_ref, ids_ref, weight_ref,
     fisher, store, grads, hidden, spread, lhs, total, turned,
-    send_sems, recv_sems, fisher_sems, store_sem,
+    send_sems, recv_sems, input_sems, fisher_sems, store_sem,
 ):
     nq, layers, _, width = factors_ref.shape
     rank = width // 2
     rows = rank * rank // LANES
     n = grads.shape[1]
     m = n * nq
-    per = hidden.shape[3] // LANES
     train = out_ref.shape[1]
 
     gathers = [
@@ -165,17 +165,34 @@
         pl.semaphore_signal(
             barrier, inc=1, device_id={"blk": peer}, device_id_type=pl.DeviceIdType.MESH
         )
+    inputs = [
+        pltpu.make_async_copy(source, target, input_sems.at[i])
+        for i, (source, target) in enumerate(
+            (
+                (factors_hbm, factors_ref),
+                (mask_hbm, mask_ref),
+                (ids_hbm, ids_ref),
+                (weight_hbm, weight_ref),
+            )
+        )
+    ]
+    for one in inputs:
+        one.start()
     fisher_copies = [
         pltpu.make_async_copy(fisher_hbm.at[l], fisher.at[l], fisher_sems.at[l])
         for l in range(layers)
     ]
     for one in fisher_copies:
         one.start()
-    for fb in range(store.shape[0]):
+    cols = store.shape[2]
+    pairs = store_hbm.reshape(train * layers, store_hbm.shape[2])
+    for slot in range(n):
         pltpu.make_async_copy(
-            store_hbm.at[:, :, fb * LANES : (fb + 1) * LANES], store.at[fb], store_sem
+            pairs.at[:, slot * cols : (slot + 1) * cols], store.at[slot], store_sem
         ).start()
 
+    for one in inputs[:2]:
+        one.wait()
     row = lax.broadcasted_iota(jnp.int32, (rows, width), 0)
     lane = lax.broadcasted_iota(jnp.int32, (rows, width), 1)
     picks = [(lane == 2 * row + par).astype(jnp.bfloat16) for par in range(2)]
@@ -199,6 +216,8 @@
         if l == 0:
             pl.semaphore_wait(barrier, len(peers))
         gathers[0][l].start()
+    for one in inputs[2:]:
+        one.wait()
     ids = ids_ref[...]
     scale = jnp.zeros(ids.shape, jnp.float32)
     for source in range(weight_ref.shape[0]):
@@ -242,12 +261,10 @@
         gathers[1][l].start()
 
     pltpu.make_async_copy(store, store, store_sem).wait()
-    flat = store.reshape(store.shape[0], train * layers, LANES)
 
     def add(slot, fresh=False):
         left = jnp.concatenate([hidden[l, slot] for l in range(layers)], axis=0)
-        right = jnp.concatenate([flat[slot * per + i] for i in range(per)], axis=1)
-        term = lax.dot_general(left, right, NT, preferred_element_type=jnp.float32)
+        term = lax.dot_general(left, store[slot], NT, preferred_element_type=jnp.float32)
         total[...] = term if fresh else total[...] + term
 
     add(me, True)
@@ -296,17 +313,18 @@
     ys = 2 if n % 4 == 0 else 1
     sizes = (n // (cores * ys), ys, cores)
     anyspace = pl.BlockSpec(memory_space=pl.ANY)
-    vmem = pl.BlockSpec(memory_space=pltpu.VMEM)
     return pl.pallas_call(
         functools.partial(kernel, sizes),
         out_shape=pltpu.VMEM((m, train), jnp.float32),
-        in_specs=[
-            vmem, vmem, vmem, pl.BlockSpec(memory_space=pltpu.SMEM), anyspace, anyspace
-        ],
-        out_specs=vmem,
+        in_specs=[anyspace] * 6,
+        out_specs=pl.BlockSpec(memory_space=pltpu.VMEM),
         scratch_shapes=[
+            pltpu.VMEM(token_mask.shape, token_mask.dtype),
+            pltpu.VMEM(factors.shape, factors.dtype),
+            pltpu.VMEM((1, train), source_ids.dtype),
+            pltpu.SMEM(source_weight.shape, source_weight.dtype),
             pltpu.VMEM((layers, cols, feat), jnp.bfloat16),
-            pltpu.VMEM((rows, train, layers, LANES), jnp.bfloat16),
+            pltpu.VMEM((n, train * layers, cols), jnp.bfloat16),
             pltpu.VMEM((layers, n, nq * rows, LANES), jnp.bfloat16),
             pltpu.VMEM((layers, n, m, cols), jnp.bfloat16),
             pltpu.VMEM((layers, rows * m, LANES), jnp.float32),
@@ -315,6 +333,7 @@
             pltpu.VMEM((train * layers, LANES), jnp.float32),
             pltpu.SemaphoreType.DMA((2, layers, n)),
             pltpu.SemaphoreType.DMA((2, layers, n)),
+            pltpu.SemaphoreType.DMA((4,)),
             pltpu.SemaphoreType.DMA((layers,)),
             pltpu.SemaphoreType.DMA(()),
         ],

time: 27.1 us -> 25.5 us (0.941)
  Pallas kernels: 26.3 us -> 24.7 us
    pallas_call x1, Pallas kernels: 26.3 us -> 24.7 us  [fused(): pl.pallas_call(functools.partial(kernel, sizes), out_shape=pltpu.VMEM((m,...]
where the time goes in v1:
time: 25.5 us; the launch traced here: 25.4 us
  Pallas kernels  24.7 us (97%)
  local copies, waits for them, and re-layouts  0.63 us (2%)
    pallas_call x1, Pallas kernels, fused(): pl.pallas_call(functools.partial(kernel, sizes), out_shape=pltpu.VMEM((m,...  24.7 us
    unnamed x1, local copies, waits for them, and re-layouts  0.63 us

profile of v1, /device:TPU:0, one launch (start us, length us, event | category | flops | bytes accessed | tf_op | source)
XLA Modules:
  0.0 25.4 jit_solution(27277121065348103)
XLA Ops:
  0.0 24.7 %scores.1 = f32[32,512]{1,0:T(8,128)S(1)} custom-call(s32[2,64]{1,0:T(2,128)} %mask_hbm.1, bf16[2,2,64,128]{3,2,1,0:T(8,128)(2,1)} %factors_hbm.1, s32[1,512]{1,0:T(1,128)} %bitcast.1, f32[16]{0:T(128)} %weight_hbm.1, bf16[2,256,4096]{2,1,0:T(8,128)(2,1)} %fisher_hbm.1, bf16[512,2,4096]{2,1,0:T(2,128)(2,1)} %store_hbm.1), custom_call_target="tpu_custom_call" | custom-call | tf_op jit(solution)/shard_map/scores/pallas_call | solution.py:316
  24.8 0.6 %copy.8 = f32[32,512]{1,0:T(8,128)} copy(f32[32,512]{1,0:T(8,128)S(1)} %scores.1) | data formatting | bytes 131072

commit v2 on v1

--- a/solution.py
+++ b/solution.py
@@ -7,6 +7,7 @@
 from jax.sharding import PartitionSpec as P
 
 LANES = 128
+DIRECT = 0
 NT = (((1,), (1,)), ((), ()))
 
 
@@ -58,7 +59,17 @@
         self.c = lax.rem(me, self.cores)
         self.y = lax.rem(me // self.cores, self.ys)
         self.z = me // (self.cores * self.ys)
-        self.sent = []
+        zs, ys, cs = (range(1, size) for size in sizes)
+        self.z_peers = [self.index(k, 0, 0) for k in zs]
+        self.y_peers = [self.index(0, j, 0) for j in ys]
+        self.c_peers = [self.index(0, 0, i) for i in cs]
+        self.across = [self.index(0, j, i) for j in ys for i in cs]
+        self.slots = {
+            (k, j, i): self.index(k, j, i)
+            for k in range(self.outer)
+            for j in range(self.ys)
+            for i in range(self.cores)
+        }
 
     def index(self, dz, dy, dc):
         if self.outer & (self.outer - 1):
@@ -73,91 +84,70 @@
         c = lax.rem(self.c + dc, self.cores)
         return (z * self.ys + y) * self.cores + c
 
-    def copy(self, slot, target, count):
+    def peers(self):
+        across = self.across if DIRECT else []
+        return self.z_peers + self.y_peers + self.c_peers + across
+
+    def direct(self, k):
+        return k >= self.outer - DIRECT
+
+    def copy(self, slot, l, target):
+        block = self.buf.at[slot, l]
         return pltpu.make_async_remote_copy(
-            src_ref=self.buf.at[slot],
-            dst_ref=self.buf.at[slot],
-            send_sem=self.send_sems.at[count],
-            recv_sem=self.recv_sems.at[slot],
+            src_ref=block,
+            dst_ref=block,
+            send_sem=self.send_sems.at[l],
+            recv_sem=self.recv_sems.at[l, slot],
             device_id={"blk": target},
             device_id_type=pl.DeviceIdType.MESH,
         )
 
-    def send(self, slot, target):
-        one = self.copy(slot, target, len(self.sent))
-        one.start()
-        self.sent.append(one)
-
-    def arrive(self, slot):
-        self.copy(slot, self.me, 0).wait_recv()
-
-    def z_peers(self):
-        return [self.index(k, 0, 0) for k in range(self.outer - 1, 0, -1)]
-
-    def y_peers(self):
-        return [self.index(0, k, 0) for k in range(1, self.ys)]
-
-    def c_peers(self):
-        return [self.index(0, 0, k) for k in range(1, self.cores)]
-
-    def peers(self):
-        return self.z_peers() + self.y_peers() + self.c_peers()
-
-    def start(self):
-        for target in self.z_peers() + self.y_peers() + self.c_peers():
-            self.send(self.me, target)
-
-    def z_slots(self):
-        return [self.index(k, 0, 0) for k in range(1, self.outer)]
-
-    def y_slots(self):
-        return [self.index(k, j, 0) for k in range(self.outer) for j in range(1, self.ys)]
-
-    def c_slots(self, near):
-        return [
-            self.index(k, j, i)
-            for i in range(1, self.cores)
-            for j in range(self.ys)
-            for k in range(self.outer)
-            if (j == 0) == near
-        ]
-
-    def take_z(self, slot):
-        self.arrive(slot)
-        for target in self.y_peers() + self.c_peers():
-            self.send(slot, target)
-
-    def take_y(self, slot):
-        self.arrive(slot)
-        for target in self.c_peers():
-            self.send(slot, target)
+    def plane(self, k, slot, l):
+        for target in self.y_peers + (self.across if self.direct(k) else []) + self.c_peers:
+            self.copy(slot, l, target).start()
+
+    def start(self, l):
+        for target in self.z_peers[::-1]:
+            self.copy(self.me, l, target).start()
+        self.plane(0, self.me, l)
+
+    def arrive(self, slot, l):
+        self.copy(slot, l, self.me).wait_recv()
+
+    def take_z(self, k, l):
+        slot = self.slots[k, 0, 0]
+        self.arrive(slot, l)
+        self.plane(k, slot, l)
+
+    def take_y(self, k, j, l):
+        slot = self.slots[k, j, 0]
+        self.arrive(slot, l)
+        if not self.direct(k):
+            for target in self.c_peers:
+                self.copy(slot, l, target).start()
 
     def finish(self):
-        for one in self.sent:
-            one.wait_send()
+        for l in range(self.buf.shape[1]):
+            sent = self.buf.at[: self.buf.shape[0] - 1, l]
+            pltpu.make_async_copy(sent, sent, self.send_sems.at[l]).wait()
 
 
 def kernel(
     sizes, mask_hbm, factors_hbm, ids_hbm, weight_hbm, fisher_hbm, store_hbm, out_ref,
     mask_ref, factors_ref, ids_ref, weight_ref,
-    fisher, store, grads, hidden, spread, lhs, total, turned,
-    send_sems, recv_sems, input_sems, fisher_sems, store_sem,
+    fisher, store, grads, hidden, spread, total, turned,
+    send_sems, recv_sems, input_sems, fisher_sem, store_sem,
 ):
     nq, layers, _, width = factors_ref.shape
     rank = width // 2
     rows = rank * rank // LANES
-    n = grads.shape[1]
+    n = grads.shape[0]
     m = n * nq
+    cols = store.shape[2]
     train = out_ref.shape[1]
 
-    gathers = [
-        [
-            Gather(buf.at[l], send_sems.at[p, l], recv_sems.at[p, l], sizes)
-            for l in range(layers)
-        ]
-        for p, buf in enumerate((grads, hidden))
-    ]
-    first = gathers[0][0]
+    first = Gather(grads, send_sems.at[0], recv_sems.at[0], sizes)
+    second = Gather(hidden, send_sems.at[1], recv_sems.at[1], sizes)
     me = first.me
     barrier = pltpu.get_barrier_semaphore()
     peers = first.peers()
@@ -178,21 +168,9 @@
     ]
     for one in inputs:
         one.start()
-    fisher_copies = [
-        pltpu.make_async_copy(fisher_hbm.at[l], fisher.at[l], fisher_sems.at[l])
-        for l in range(layers)
-    ]
-    for one in fisher_copies:
-        one.start()
-    cols = store.shape[2]
-    pairs = store_hbm.reshape(train * layers, store_hbm.shape[2])
-    for slot in range(n):
-        pltpu.make_async_copy(
-            pairs.at[:, slot * cols : (slot + 1) * cols], store.at[slot], store_sem
-        ).start()
-
     for one in inputs[:2]:
         one.wait()
+
     row = lax.broadcasted_iota(jnp.int32, (rows, width), 0)
     lane = lax.broadcasted_iota(jnp.int32, (rows, width), 1)
     picks = [(lane == 2 * row + par).astype(jnp.bfloat16) for par in range(2)]
@@ -212,10 +190,17 @@
                 left = (left * keep).astype(jnp.bfloat16)
                 term = jnp.dot(left, rights[par], preferred_element_type=jnp.float32)
                 grad = term if grad is None else grad + term
-            grads[l, me, q * rows : (q + 1) * rows, :] = grad.astype(jnp.bfloat16)
+            grads[me, l, q * rows : (q + 1) * rows, :] = grad.astype(jnp.bfloat16)
         if l == 0:
             pl.semaphore_wait(barrier, len(peers))
-        gathers[0][l].start()
+        first.start(l)
+
+    pltpu.make_async_copy(fisher_hbm, fisher, fisher_sem).start()
+    pairs = store_hbm.reshape(train * layers, store_hbm.shape[2])
+    for slot in range(n):
+        pltpu.make_async_copy(
+            pairs.at[:, slot * cols : (slot + 1) * cols], store.at[slot], store_sem
+        ).start()
     for one in inputs[2:]:
         one.wait()
     ids = ids_ref[...]
@@ -223,74 +208,73 @@
     for source in range(weight_ref.shape[0]):
         scale = scale + jnp.where(ids == source, weight_ref[source], 0.0)
 
-    def place(l, slot):
+    def place(slot, l):
         for q in range(nq):
             spread[l, pl.ds(slot * nq + q, rows, stride=m), :] = grads[
-                l, slot, q * rows : (q + 1) * rows, :
+                slot, l, q * rows : (q + 1) * rows, :
             ].astype(jnp.float32)
 
-    for l in range(layers):
-        place(l, me)
-    for l in range(layers):
-        one = gathers[0][l]
-        for slot in one.z_slots():
-            one.take_z(slot)
-            place(l, slot)
-    for l in range(layers):
-        one = gathers[0][l]
-        for slot in one.y_slots():
-            one.take_y(slot)
-            place(l, slot)
-    for l in range(layers):
-        one = gathers[0][l]
-        for slot in one.c_slots(True):
-            one.arrive(slot)
-            place(l, slot)
-
-    for l in range(layers):
-        for slot in gathers[0][l].c_slots(False):
-            gathers[0][l].arrive(slot)
-            place(l, slot)
-        for r in range(rows):
-            lhs[:, r * LANES : (r + 1) * LANES] = spread[l, r * m : (r + 1) * m, :].astype(
-                jnp.bfloat16
-            )
-        fisher_copies[l].wait()
-        product = lax.dot_general(lhs[...], fisher[l], NT, preferred_element_type=jnp.float32)
-        hidden[l, me] = product.astype(jnp.bfloat16)
-        gathers[1][l].start()
+    def precondition(l):
+        left = jnp.concatenate(
+            [spread[l, r * m : (r + 1) * m, :].astype(jnp.bfloat16) for r in range(rows)], axis=1
+        )
+        if l == 0:
+            pltpu.make_async_copy(fisher_hbm, fisher, fisher_sem).wait()
+        half = fisher.shape[2] // 2
+        product = lax.dot_general(
+            left[:, :half], fisher[l, :, :half], NT, preferred_element_type=jnp.float32
+        ) + lax.dot_general(
+            left[:, half:], fisher[l, :, half:], NT, preferred_element_type=jnp.float32
+        )
+        hidden[me, l] = product.astype(jnp.bfloat16)
+        second.start(l)
+
+    for l in range(layers):
+        place(me, l)
+    outer, ys, cores = sizes
+    flat = [(k, j) for k in range(outer) for j in range(1, ys)]
+    ends = [(k, j, i) for j in range(ys) for k in range(outer) for i in range(1, cores)]
+    for l in range(layers):
+        for k in range(1, outer):
+            first.take_z(k, l)
+            place(first.slots[k, 0, 0], l)
+    for l in range(layers):
+        for k, j in flat:
+            first.take_y(k, j, l)
+            place(first.slots[k, j, 0], l)
+    for l in range(layers):
+        for at in ends:
+            first.arrive(first.slots[at], l)
+            place(first.slots[at], l)
+        precondition(l)
 
     pltpu.make_async_copy(store, store, store_sem).wait()
 
     def add(slot, fresh=False):
-        left = jnp.concatenate([hidden[l, slot] for l in range(layers)], axis=0)
+        left = jnp.concatenate([hidden[slot, l] for l in range(layers)], axis=0)
         term = lax.dot_general(left, store[slot], NT, preferred_element_type=jnp.float32)
         total[...] = term if fresh else total[...] + term
 
     add(me, True)
-    pair = gathers[1]
-    slots = pair[0].z_slots()
-    for one in pair[:-1]:
-        for slot in slots:
-            one.take_z(slot)
-    for slot in slots:
-        pair[-1].take_z(slot)
-        add(slot)
-    early = pair[0].c_slots(True)
-    slots = pair[0].y_slots()
-    for at in range(max(len(slots), len(early))):
-        for slot in slots[at : at + 1]:
-            for one in pair:
-                one.take_y(slot)
-            add(slot)
-        for slot in early[at : at + 1]:
-            for one in pair:
-                one.arrive(slot)
-            add(slot)
-    for slot in pair[0].c_slots(False):
-        for one in pair:
-            one.arrive(slot)
-        add(slot)
+    for l in range(layers):
+        for k in range(1, outer):
+            second.take_z(k, l)
+            if l == layers - 1:
+                add(second.slots[k, 0, 0])
+    early = ends[: outer * (cores - 1)]
+    for at in range(max(len(flat), len(early))):
+        for k, j in flat[at : at + 1]:
+            for l in range(layers):
+                second.take_y(k, j, l)
+            add(second.slots[k, j, 0])
+        for where in early[at : at + 1]:
+            for l in range(layers):
+                second.arrive(second.slots[where], l)
+            add(second.slots[where])
+    for where in ends[len(early) :]:
+        for l in range(layers):
+            second.arrive(second.slots[where], l)
+        add(second.slots[where])
 
     turned[:, : layers * m] = total[...].T
     answer = None
@@ -298,9 +282,8 @@
         part = turned[pl.ds(l, train, stride=layers), :][:, l * m : (l + 1) * m]
         answer = part if answer is None else answer + part
     out_ref[...] = answer.T * scale
-    for some in gathers:
-        for one in some:
-            one.finish()
+    first.finish()
+    second.finish()
 
 
 def fused(n, factors, token_mask, store, inv_fisher, source_ids, source_weight):
@@ -325,16 +308,15 @@
             pltpu.SMEM(source_weight.shape, source_weight.dtype),
             pltpu.VMEM((layers, cols, feat), jnp.bfloat16),
             pltpu.VMEM((n, train * layers, cols), jnp.bfloat16),
-            pltpu.VMEM((layers, n, nq * rows, LANES), jnp.bfloat16),
-            pltpu.VMEM((layers, n, m, cols), jnp.bfloat16),
+            pltpu.VMEM((n, layers, nq * rows, LANES), jnp.bfloat16),
+            pltpu.VMEM((n, layers, m, cols), jnp.bfloat16),
             pltpu.VMEM((layers, rows * m, LANES), jnp.float32),
-            pltpu.VMEM((m, feat), jnp.bfloat16),
             pltpu.VMEM((layers * m, train * layers), jnp.float32),
             pltpu.VMEM((train * layers, LANES), jnp.float32),
-            pltpu.SemaphoreType.DMA((2, layers, n)),
+            pltpu.SemaphoreType.DMA((2, layers)),
             pltpu.SemaphoreType.DMA((2, layers, n)),
             pltpu.SemaphoreType.DMA((4,)),
-            pltpu.SemaphoreType.DMA((layers,)),
+            pltpu.SemaphoreType.DMA(()),
             pltpu.SemaphoreType.DMA(()),
         ],
         compiler_params=pltpu.CompilerParams(

time: 25.5 us -> 24.8 us (0.973)
  Pallas kernels: 24.7 us -> 24 us
    pallas_call x1, Pallas kernels: 24.7 us -> 24 us  [fused(): pl.pallas_call(functools.partial(kernel, sizes), out_shape=pltpu.VMEM((m,...]
where the time goes in v2:
time: 24.8 us; the launch traced here: 24.7 us
  Pallas kernels  24 us (97%)
  local copies, waits for them, and re-layouts  0.63 us (3%)
    pallas_call x1, Pallas kernels, fused(): pl.pallas_call(functools.partial(kernel, sizes), out_shape=pltpu.VMEM((m,...  24 us
    unnamed x1, local copies, waits for them, and re-layouts  0.63 us

profile of v2, /device:TPU:0, one launch (start us, length us, event | category | flops | bytes accessed | tf_op | source)
XLA Modules:
  0.0 24.7 jit_solution(17264583483416488368)
XLA Ops:
  0.0 24.0 %scores.1 = f32[32,512]{1,0:T(8,128)S(1)} custom-call(s32[2,64]{1,0:T(2,128)} %mask_hbm.1, bf16[2,2,64,128]{3,2,1,0:T(8,128)(2,1)} %factors_hbm.1, s32[1,512]{1,0:T(1,128)} %bitcast.1, f32[16]{0:T(128)} %weight_hbm.1, bf16[2,256,4096]{2,1,0:T(8,128)(2,1)} %fisher_hbm.1, bf16[512,2,4096]{2,1,0:T(2,128)(2,1)} %store_hbm.1), custom_call_target="tpu_custom_call" | custom-call | tf_op jit(solution)/shard_map/scores/pallas_call | solution.py:299
  24.0 0.6 %copy.8 = f32[32,512]{1,0:T(8,128)} copy(f32[32,512]{1,0:T(8,128)S(1)} %scores.1) | data formatting | bytes 131072

commit v3 on v2

--- a/solution.py
+++ b/solution.py
@@ -7,7 +7,6 @@
 from jax.sharding import PartitionSpec as P
 
 LANES = 128
-DIRECT = 0
 NT = (((1,), (1,)), ((), ()))
 
 
@@ -63,7 +62,11 @@
         self.z_peers = [self.index(k, 0, 0) for k in zs]
         self.y_peers = [self.index(0, j, 0) for j in ys]
         self.c_peers = [self.index(0, 0, i) for i in cs]
-        self.across = [self.index(0, j, i) for j in ys for i in cs]
+        self.far_first = self.z_peers[::-1]
+        if self.outer == 4:
+            inner = lax.rem(self.z + self.z // 2, 2) == 1
+            near, b, c = self.z_peers
+            self.far_first = [jnp.where(inner, b, c), jnp.where(inner, c, b), near]
         self.slots = {
             (k, j, i): self.index(k, j, i)
             for k in range(self.outer)
@@ -85,11 +88,7 @@
         return (z * self.ys + y) * self.cores + c
 
     def peers(self):
-        across = self.across if DIRECT else []
-        return self.z_peers + self.y_peers + self.c_peers + across
-
-    def direct(self, k):
-        return k >= self.outer - DIRECT
+        return self.z_peers + self.y_peers + self.c_peers
 
     def copy(self, slot, l, target):
         block = self.buf.at[slot, l]
@@ -102,14 +101,14 @@
             device_id_type=pl.DeviceIdType.MESH,
         )
 
-    def plane(self, k, slot, l):
-        for target in self.y_peers + (self.across if self.direct(k) else []) + self.c_peers:
+    def plane(self, slot, l):
+        for target in self.y_peers + self.c_peers:
             self.copy(slot, l, target).start()
 
     def start(self, l):
-        for target in self.z_peers[::-1]:
+        for target in self.far_first:
             self.copy(self.me, l, target).start()
-        self.plane(0, self.me, l)
+        self.plane(self.me, l)
 
     def arrive(self, slot, l):
         self.copy(slot, l, self.me).wait_recv()
@@ -117,14 +116,13 @@
     def take_z(self, k, l):
         slot = self.slots[k, 0, 0]
         self.arrive(slot, l)
-        self.plane(k, slot, l)
+        self.plane(slot, l)
 
     def take_y(self, k, j, l):
         slot = self.slots[k, j, 0]
         self.arrive(slot, l)
-        if not self.direct(k):
-            for target in self.c_peers:
-                self.copy(slot, l, target).start()
+        for target in self.c_peers:
+            self.copy(slot, l, target).start()
 
     def finish(self):
         for l in range(self.buf.shape[1]):
@@ -195,40 +193,38 @@
             pl.semaphore_wait(barrier, len(peers))
         first.start(l)
 
+    for one in inputs[2:]:
+        one.wait()
+    ids = ids_ref[...]
+    scale = jnp.zeros(ids.shape, jnp.float32)
+    for source in range(weight_ref.shape[0]):
+        scale = scale + jnp.where(ids == source, weight_ref[source], 0.0)
+
+    def place(slot, l):
+        for q in range(nq):
+            spread[l, pl.ds(slot * nq + q, rows, stride=m), :] = grads[
+                slot, l, q * rows : (q + 1) * rows, :
+            ].astype(jnp.float32)
+
+    def precondition(l):
+        left = jnp.concatenate(
+            [spread[l, r * m : (r + 1) * m, :].astype(jnp.bfloat16) for r in range(rows)], axis=1
+        )
+        if l == 0:
+            pltpu.make_async_copy(fisher_hbm, fisher, fisher_sem).wait()
+        for at in range(0, cols, LANES):
+            product = lax.dot_general(
+                left, fisher[l, at : at + LANES], NT, preferred_element_type=jnp.float32
+            )
+            hidden[me, l, :, at : at + LANES] = product.astype(jnp.bfloat16)
+        second.start(l)
+
     pltpu.make_async_copy(fisher_hbm, fisher, fisher_sem).start()
     pairs = store_hbm.reshape(train * layers, store_hbm.shape[2])
     for slot in range(n):
         pltpu.make_async_copy(
             pairs.at[:, slot * cols : (slot + 1) * cols], store.at[slot], store_sem
         ).start()
-    for one in inputs[2:]:
-        one.wait()
-    ids = ids_ref[...]
-    scale = jnp.zeros(ids.shape, jnp.float32)
-    for source in range(weight_ref.shape[0]):
-        scale = scale + jnp.where(ids == source, weight_ref[source], 0.0)
-
-    def place(slot, l):
-        for q in range(nq):
-            spread[l, pl.ds(slot * nq + q, rows, stride=m), :] = grads[
-                slot, l, q * rows : (q + 1) * rows, :
-            ].astype(jnp.float32)
-
-    def precondition(l):
-        left = jnp.concatenate(
-            [spread[l, r * m : (r + 1) * m, :].astype(jnp.bfloat16) for r in range(rows)], axis=1
-        )
-        if l == 0:
-            pltpu.make_async_copy(fisher_hbm, fisher, fisher_sem).wait()
-        half = fisher.shape[2] // 2
-        product = lax.dot_general(
-            left[:, :half], fisher[l, :, :half], NT, preferred_element_type=jnp.float32
-        ) + lax.dot_general(
-            left[:, half:], fisher[l, :, half:], NT, preferred_element_type=jnp.float32
-        )
-        hidden[me, l] = product.astype(jnp.bfloat16)
-        second.start(l)
-
     for l in range(layers):
         place(me, l)
     outer, ys, cores = sizes
@@ -276,10 +272,15 @@
             second.arrive(second.slots[where], l)
         add(second.slots[where])
 
-    turned[:, : layers * m] = total[...].T
+    scores = total[...]
+    layer = lax.rem(lax.broadcasted_iota(jnp.int32, (m, scores.shape[1]), 1), layers)
+    own = scores[:m]
+    for l in range(1, layers):
+        own = jnp.where(layer == l, scores[l * m : (l + 1) * m], own)
+    turned[:, :m] = own.T
     answer = None
     for l in range(layers):
-        part = turned[pl.ds(l, train, stride=layers), :][:, l * m : (l + 1) * m]
+        part = turned[pl.ds(l, train, stride=layers), :][:, :m]
         answer = part if answer is None else answer + part
     out_ref[...] = answer.T * scale
     first.finish()

time: 24.8 us -> 24.1 us (0.972)
  Pallas kernels: 24 us -> 23.3 us
    pallas_call x1, Pallas kernels: 24 us -> 23.3 us  [fused(): pl.pallas_call(functools.partial(kernel, sizes), out_shape=pltpu.VMEM((m,...]
where the time goes in v3:
time: 24.1 us; the launch traced here: 24 us
  Pallas kernels  23.3 us (97%)
  local copies, waits for them, and re-layouts  0.63 us (3%)
    pallas_call x1, Pallas kernels, fused(): pl.pallas_call(functools.partial(kernel, sizes), out_shape=pltpu.VMEM((m,...  23.3 us
    unnamed x1, local copies, waits for them, and re-layouts  0.63 us

profile of v3, /device:TPU:0, one launch (start us, length us, event | category | flops | bytes accessed | tf_op | source)
XLA Modules:
  0.0 24.0 jit_solution(15941137501380036562)
XLA Ops:
  0.0 23.3 %scores.1 = f32[32,512]{1,0:T(8,128)S(1)} custom-call(s32[2,64]{1,0:T(2,128)} %mask_hbm.1, bf16[2,2,64,128]{3,2,1,0:T(8,128)(2,1)} %factors_hbm.1, s32[1,512]{1,0:T(1,128)} %bitcast.1, f32[16]{0:T(128)} %weight_hbm.1, bf16[2,256,4096]{2,1,0:T(8,128)(2,1)} %fisher_hbm.1, bf16[512,2,4096]{2,1,0:T(2,128)(2,1)} %store_hbm.1), custom_call_target="tpu_custom_call" | custom-call | tf_op jit(solution)/shard_map/scores/pallas_call | solution.py:300
  23.3 0.6 %copy.8 = f32[32,512]{1,0:T(8,128)} copy(f32[32,512]{1,0:T(8,128)S(1)} %scores.1) | data formatting | bytes 131072
